TPU v7x, 32 devices: a whole 2x2x4 slice. The times are simulated.
32 devices in a mesh: groups: 2 (over x), view: 16 (over z, y, core).
Axes of the slice: x: 2, y: 2, z: 4, core: 2. Of those that a mesh axis runs over, the one named last changes fastest.
Arguments:
- materials: float32 [3, 64, 256, 512], P(None, ('groups', 'view')), parts along dimension 1, as said below
- column_profile: bfloat16 [2, 512, 1280], replicated, as said below
- row_profile: bfloat16 [2, 256, 1280], replicated, as said below
- start_block: int32 [32], P(('groups', 'view')), parts along dimension 0, may hold values from 0 to 30, as said below
- block_count: int32 [32], P(('groups', 'view')), parts along dimension 0, may hold values from 1 to 4, as said below
- tile_ids: int32 [32, 4], P(('groups', 'view')), parts along dimension 0, may hold values from 0 to 1
- photon_counts: int32 [32, 8, 4, 1280], P(('groups', 'view')), parts along dimension 0, may hold values from 0 to 3199
- spectrum: float32 [8, 16], replicated, may hold values from 20 to 200
- attenuation: float32 [16, 3], replicated, may hold values from 0.05 to 0.5
- step_size: float32 [3], replicated, may hold values from 0.002 to 0.01
Outputs:
- updated: float32 [3, 64, 256, 512], P(None, ('groups', 'view')), parts along dimension 1
There are 2 independent parts, one for each index of `groups`. A program takes and returns all parts, laid end to end along the dimension named above; an argument that names none is the same for every part. Nothing has to cross between parts.
Inputs may be any that keep to these rules, and one draw needn't show every extreme that they name: `start_block`: every slice of a view's window lies among the 2 slices of the device that holds the view (view v belongs to device v) and the 2 slices on either side; the window ends at or before slice 32 - 1. `block_count`: windows of views are ragged; some view of every scan covers 4 slices. `column_profile`: entries are non-negative and below 1. `row_profile`: entries are non-negative and below 1. `materials`: entries lie between 0 and 1.
All inputs are finite; a program needn't handle non-finite values.
Results may differ from a plain program's by a relative error of at most 0.00057.
Values may be sent and summed in bfloat16 or wider, within the bound.
A program may use at most 64 MiB of HBM per device.

v0:
```python
import jax
import jax.numpy as jnp
from jax import lax
from jax.sharding import PartitionSpec as P

ITERS = 2


def extended_2(block, sides, width):
    for axis, dim in sides:
        count = lax.axis_size(axis)
        forward = [(i, i + 1) for i in range(count - 1)]
        backward = [(target, source) for source, target in forward]
        low = lax.ppermute(
            lax.slice_in_dim(block, block.shape[dim] - width, None, axis=dim), axis, forward
        )
        high = lax.ppermute(lax.slice_in_dim(block, 0, width, axis=dim), axis, backward)
        block = jnp.concatenate([low, block, high], axis=dim)
    return block


def shifted(x, axis, by):
    size = lax.axis_size(axis)
    pairs = [(i, i + by) for i in range(size) if 0 <= i + by < size]
    return lax.ppermute(x, axis, pairs)


def poisson_gradient(line, counts, rowmask, spectrum, attenuation):
    highest = lax.Precision.HIGHEST
    atten_sum = jnp.einsum("km,vmrp->vkrp", attenuation, line, precision=highest)
    trans = jnp.exp(-atten_sum)
    expected = jnp.einsum("ek,vkrp->verp", spectrum, trans, precision=highest)
    weight = 1.0 - counts.astype(jnp.float32) / expected
    back_terms = jnp.einsum("ek,verp->vkrp", spectrum, weight, precision=highest)
    grad_full = -jnp.einsum("km,vkrp->vmrp", attenuation, trans * back_terms, precision=highest)
    return (grad_full * rowmask[:, None, :, None]).astype(jnp.bfloat16)


def local(
    materials,
    column_profile,
    row_profile,
    start_block,
    block_count,
    tile_ids,
    photon_counts,
    spectrum,
    attenuation,
    step_size,
):
    mats, own_blocks, image_rows, image_cols = materials.shape
    columns = column_profile.shape[2]
    views_here, window = tile_ids.shape
    slots_all = views_here * window
    base_block = lax.axis_index("view") * own_blocks - own_blocks
    slot_numbers = jnp.arange(slots_all)
    slot_view = slot_numbers // window
    slot_pos = slot_numbers % window
    local_block = jnp.clip(start_block[slot_view] - base_block + slot_pos, 0, 3 * own_blocks - 1)
    slot_valid = slot_pos < block_count[slot_view]
    slot_tile = tile_ids.reshape(slots_all)
    row_slot = jnp.arange(window)
    rowmask = (row_slot[None, :] < block_count[:, None]).astype(jnp.float32)
    for iteration in range(ITERS):
        rounded = materials.astype(jnp.bfloat16)
        extended = extended_2(rounded, (("view", 1),), own_blocks)

        def project(slot_index):
            col_tile = lax.dynamic_index_in_dim(
                column_profile, slot_tile[slot_index], 0, keepdims=False
            )
            row_tile = lax.dynamic_index_in_dim(
                row_profile, slot_tile[slot_index], 0, keepdims=False
            )
            block_data = lax.dynamic_index_in_dim(
                extended, local_block[slot_index], 1, keepdims=False
            )

            def project_compute(unused):
                across = jnp.dot(
                    block_data.reshape(mats * image_rows, image_cols),
                    col_tile,
                    preferred_element_type=jnp.float32,
                )
                return jnp.sum(
                    across.reshape(mats, image_rows, columns) * row_tile.astype(jnp.float32)[None],
                    axis=1,
                )

            return lax.cond(
                slot_valid[slot_index],
                project_compute,
                lambda unused: jnp.zeros((mats, columns), jnp.float32),
                0,
            )

        pieces = lax.map(project, slot_numbers)
        line = pieces.reshape(views_here, window, mats, columns).transpose(0, 2, 1, 3)
        gradient = poisson_gradient(line, photon_counts, rowmask, spectrum, attenuation)
        grad_slots = gradient.transpose(0, 2, 1, 3).reshape(slots_all, mats, columns)

        def accumulate(summed, slot_index):
            col_tile = lax.dynamic_index_in_dim(
                column_profile, slot_tile[slot_index], 0, keepdims=False
            )
            row_tile = lax.dynamic_index_in_dim(
                row_profile, slot_tile[slot_index], 0, keepdims=False
            )
            grad_rows = grad_slots[slot_index].astype(jnp.float32)
            where = local_block[slot_index]

            def accumulate_compute(unused):
                weighted = (grad_rows[:, None, :] * row_tile.astype(jnp.float32)[None]).astype(
                    jnp.bfloat16
                )
                return lax.dot_general(
                    weighted.reshape(mats * image_rows, columns),
                    col_tile,
                    (((1,), (1,)), ((), ())),
                    preferred_element_type=jnp.float32,
                ).reshape(mats, image_rows, image_cols)

            current = lax.dynamic_index_in_dim(summed, where, 1, keepdims=False)
            added = lax.cond(
                slot_valid[slot_index],
                lambda unused: current + accumulate_compute(0),
                lambda unused: current,
                0,
            )
            return (lax.dynamic_update_index_in_dim(summed, added, where, 1), None)

        empty = jnp.zeros((mats, 3 * own_blocks, image_rows, image_cols), jnp.float32)
        summed, unused = lax.scan(accumulate, empty, slot_numbers)
        lower_rim = summed[:, :own_blocks]
        middle = summed[:, own_blocks : 2 * own_blocks]
        upper_rim = summed[:, 2 * own_blocks :]
        from_upper = shifted(lower_rim, "view", -1)
        from_lower = shifted(upper_rim, "view", 1)
        backprojected = middle + from_lower + from_upper
        materials = materials - step_size[:, None, None, None] * backprojected
    return materials


def solution(mesh):
    placed = (
        P(None, ("groups", "view"), None, None),
        P(),
        P(),
        P(("groups", "view")),
        P(("groups", "view")),
        P(("groups", "view"), None),
        P(("groups", "view"), None, None, None),
        P(),
        P(),
        P(),
    )
    return jax.shard_map(
        local,
        mesh=mesh,
        in_specs=placed,
        out_specs=P(None, ("groups", "view"), None, None),
        check_vma=False,
    )
```

profile of v0, /device:TPU:6, one launch (start us, length us, event | category | flops | bytes accessed | tf_op | source)
XLA Modules:
  0.0 465.2 jit_solution(16679488305764209267)
XLA Ops:
  4.0 2.4 collective-permute-start
  7.8 14.1 %collective-permute-done.1 = bf16[3,2,256,512]{3,2,0,1:T(8,128)(2,1)} collective-permute-done((bf16[3,2,256,512]{3,2,0,1:T(8,128)(2,1)S(1)}, bf16[3,2,256,512]{3,2,0,1:T(8,128)(2,1)}, u32[]{:S(2)}, u32[]{:S(2)}) %collective-permute-start.1) | collective-permute-done | bytes 1572896 | tf_op jit(solution)/shard_map/ppermute | solution.py:17
  22.0 19.8 %collective-permute-done = bf16[3,2,256,512]{3,2,0,1:T(8,128)(2,1)} collective-permute-done((bf16[3,2,256,512]{3,2,0,1:T(8,128)(2,1)S(1)}, bf16[3,2,256,512]{3,2,0,1:T(8,128)(2,1)}, u32[]{:S(2)}, u32[]{:S(2)}) %collective-permute-start) | collective-permute-done | bytes 1572896 | tf_op jit(solution)/shard_map/ppermute | solution.py:14
  41.7 5.8 %pad_maximum_fusion = bf16[3,6,256,512]{3,2,0,1:T(8,128)(2,1)} fusion(bf16[3,2,256,512]{3,2,0,1:T(8,128)(2,1)} %collective-permute-done.1, bf16[3,2,256,512]{3,2,0,1:T(8,128)(2,1)} %collective-permute-done, f32[3,2,256,512]{3,2,1,0:T(8,128)} %param.26), kind=kLoop, calls=%fused_computation.52 | loop fusion | flops 14155776 | bytes 11010048 | tf_op jit(solution)/shard_map/concatenate | solution.py:18
  47.6 22.6 %while.44 = (s32[]{:T(128)}, f32[4,3,1280]{2,1,0:T(4,128)S(1)}, s32[4]{0:T(128)S(1)}, pred[4]{0:T(512)(128)(4,1)S(1)}, bf16[3,6,256,512]{3,2,0,1:T(8,128)(2,1)},...) while((s32[]{:T(128)}, f32[4,3,1280]{2,1,0:T(4,128)S(1)}, ...), condition=%wide.region_4.5_spmd.clone, body=%wide.region_0.4_spmd.clone.sunk | while | flops 1008922944 | bytes 5430818 | solution.py:97
  51.2 8.0 %conditional.12 = (f32[1,3,1280]{2,1,0:T(4,128)S(1)}) conditional(s32[]{:T(128)} %bitcast.236, () %tuple.186, (s32[]{:T(128)}, s32[]{:T(128)}, bf16[3,6,256,512]{3,2,0,1:T(8,128)(2,1)}, s32[4]{0:T(128)S(1)}, bf16[2,512,1280]{2,1,0:T(8,128)(2,1)}, /*index=5*/bf16[2,256,1280]{2,1,0:T(8,128)(2,1)S(1)}, s32[]{:T(128)}, s32[4]{0:T(128)S(1)}, ...), branch_computations={%region_1.1_spmd, %region_2.3_spmd.clone} | conditional | flops 1008922944 | bytes 5389532 | solution.py:90
  56.4 2.8 fusion.16
  71.8 4.9 %broadcast.71.clone2 = f32[3,6,256,512]{3,2,1,0:T(8,128)} broadcast(f32[]{:T(128)} %constant.191.clone.1), dimensions={} | broadcast | bytes 9437188 | tf_op jit(solution)/shard_map/broadcast.15
  76.7 42.6 %while.42 = (s32[]{:T(128)}, f32[3,6,256,512]{3,2,1,0:T(8,128)}, s32[4]{0:T(128)S(1)}, pred[4]{0:T(512)(128)(4,1)S(1)}, s32[4]{0:T(128)S(1)}, /*index=5*/s32[4]{...) while((s32[]{:T(128)}, f32[3,6,256,512]{3,2,1,0:T(8,128)}, ...), condition=%wide.region_8.9_spmd, body=%wide.region_5.8_spmd.sunk | while | flops 1009323776 | bytes 14063462 | solution.py:133
  84.7 5.5 %conditional.10 = (f32[3,1,256,512]{3,2,0,1:T(8,128)S(1)}) conditional(s32[]{:T(128)} %bitcast.229, f32[3,256,512]{2,1,0:T(8,128)S(1)} %dynamic-slice_bitcast_fusion.4, (bf16[4,3,1280]{2,1,0:T(4,128)(2,1)S(1)}, s32[]{:T(128)}, s32[4]{0:T(128)S(1)}, bf16[2,256,1280]{2,1,0:T(8,128)(2,1)S(1)}, bf16[2,512,1280]{2,1,0:T(8,128)(2,1)}, ...), branch_computations={%region_6.6_spmd, %region_7.7_spmd.clone} | conditional | flops 1009323776 | bytes 7771714 | solution.py:124
  87.6 2.6 add_bitcast_fusion
  119.4 3.7 fusion.64
  123.1 26.3 %collective-permute-start.2 = (f32[3,2,256,512]{3,2,1,0:T(8,128)S(1)}, f32[3,2,256,512]{3,2,1,0:T(8,128)S(1)}, u32[]{:S(2)}, u32[]{:S(2)}) collective-permute-start(f32[3,2,256,512]{3,2,1,0:T(8,128)S(1)} %get-tuple-element.848), channel_id=1, source_target_pairs={{0,1},{1,2},{2,3},{3,4},{4,5},{5,6},{6,7},{7,8},{8,9},{9,10},{10,1... | collective-permute-start | bytes 9437192 | tf_op jit(solution)/shard_map/ppermute | solution.py:25
  149.4 17.0 %collective-permute-start.3 = (f32[3,2,256,512]{3,2,1,0:T(8,128)S(1)}, f32[3,2,256,512]{3,2,1,0:T(8,128)S(1)}, u32[]{:S(2)}, u32[]{:S(2)}) collective-permute-start(f32[3,2,256,512]{3,2,1,0:T(8,128)S(1)} %get-tuple-element.849), channel_id=1, source_target_pairs={{1,0},{2,1},{3,2},{4,3},{5,4},{6,5},{7,6},{8,7},{9,8},{10,9},{11,1... | collective-permute-start | bytes 9437192 | tf_op jit(solution)/shard_map/ppermute | solution.py:25
  166.4 73.8 %collective-permute-done.2 = f32[3,2,256,512]{3,2,1,0:T(8,128)S(1)} collective-permute-done((f32[3,2,256,512]{3,2,1,0:T(8,128)S(1)}, f32[3,2,256,512]{3,2,1,0:T(8,128)S(1)}, u32[]{:S(2)}, u32[]{:S(2)}) %collective-permute-start.2) | collective-permute-done | bytes 3145760 | tf_op jit(solution)/shard_map/ppermute | solution.py:25
  240.2 4.9 %fusion.62 = (bf16[3,2,256,512]{3,2,1,0:T(8,128)(2,1)S(1)}, f32[3,2,256,512]{3,2,1,0:T(8,128)}) fusion(f32[3,2,256,512]{3,2,1,0:T(8,128)S(1)} %copy-done.2, f32[3,2,256,512]{3,2,1,0:T(8,128)S(1)} %collective-permute-done.3, f32[3,2,256,512]{3,2,1,0:T(8,128)S(1)} %collective-permute-done.2, f32[3,6,256,512]{3,2,1,0:T(8,128)} %get-tuple-element.590, ...), kind=kLoop, calls=%fused_computation.102 | loop fusion | flops 3932160 | bytes 17301516 | tf_op jit(solution)/shard_map/convert_element_type | solution.py:65
  247.0 2.6 collective-permute-start.4
  249.6 15.3 %collective-permute-done.5 = bf16[3,2,256,512]{3,2,1,0:T(8,128)(2,1)} collective-permute-done((bf16[3,2,256,512]{3,2,1,0:T(8,128)(2,1)S(1)}, bf16[3,2,256,512]{3,2,1,0:T(8,128)(2,1)}, u32[]{:S(2)}, u32[]{:S(2)}) %collective-permute-start.5) | collective-permute-done | bytes 1572896 | tf_op jit(solution)/shard_map/ppermute | solution.py:17
  264.9 3.9 collective-permute-done.4
  271.0 2.5 copy.16
  273.5 23.4 %while.45 = (s32[]{:T(128)}, f32[4,3,1280]{2,1,0:T(4,128)S(1)}, s32[4]{0:T(128)S(1)}, pred[4]{0:T(512)(128)(4,1)S(1)}, bf16[3,6,256,512]{3,2,0,1:T(8,128)(2,1)},...) while((s32[]{:T(128)}, f32[4,3,1280]{2,1,0:T(4,128)S(1)}, ...), condition=%wide.region_13.14_spmd.clone, body=%wide.region_9.13_spmd.clone.sunk | while | flops 1008922944 | bytes 5430818 | solution.py:97
  277.2 8.1 %conditional.13 = (f32[1,3,1280]{2,1,0:T(4,128)S(1)}) conditional(s32[]{:T(128)} %bitcast.238, () %tuple.189, (s32[]{:T(128)}, s32[]{:T(128)}, bf16[3,6,256,512]{3,2,0,1:T(8,128)(2,1)}, s32[4]{0:T(128)S(1)}, bf16[2,512,1280]{2,1,0:T(8,128)(2,1)}, /*index=5*/bf16[2,256,1280]{2,1,0:T(8,128)(2,1)S(1)}, s32[]{:T(128)}, s32[4]{0:T(128)S(1)}, ...), branch_computations={%region_10.10_spmd, %region_11.12_spmd.clone} | conditional | flops 1008922944 | bytes 5389532 | solution.py:90
  282.5 2.8 fusion.23
  298.5 4.9 %broadcast.71.clone = f32[3,6,256,512]{3,2,1,0:T(8,128)} broadcast(f32[]{:T(128)} %constant.191.clone.1), dimensions={} | broadcast | bytes 9437188 | tf_op jit(solution)/shard_map/broadcast.15
  303.4 42.6 %while.43 = (s32[]{:T(128)}, f32[3,6,256,512]{3,2,1,0:T(8,128)}, s32[4]{0:T(128)S(1)}, pred[4]{0:T(512)(128)(4,1)S(1)}, s32[4]{0:T(128)S(1)}, /*index=5*/s32[4]{...) while((s32[]{:T(128)}, f32[3,6,256,512]{3,2,1,0:T(8,128)}, ...), condition=%wide.region_17.18_spmd, body=%wide.region_14.17_spmd.sunk | while | flops 1009323776 | bytes 14063462 | solution.py:133
  311.3 5.5 %conditional.11 = (f32[3,1,256,512]{3,2,0,1:T(8,128)S(1)}) conditional(s32[]{:T(128)} %bitcast.234, f32[3,256,512]{2,1,0:T(8,128)S(1)} %dynamic-slice_bitcast_fusion.5, (bf16[4,3,1280]{2,1,0:T(4,128)(2,1)S(1)}, s32[]{:T(128)}, s32[4]{0:T(128)S(1)}, bf16[2,256,1280]{2,1,0:T(8,128)(2,1)S(1)}, bf16[2,512,1280]{2,1,0:T(8,128)(2,1)}, ...), branch_computations={%region_15.15_spmd, %region_16.16_spmd.clone} | conditional | flops 1009323776 | bytes 7771714 | solution.py:124
  314.2 2.6 add_bitcast_fusion.1
  346.0 3.7 fusion.63
  349.7 40.5 %collective-permute-start.6 = (f32[3,2,256,512]{3,2,1,0:T(8,128)S(1)}, f32[3,2,256,512]{3,2,1,0:T(8,128)S(1)}, u32[]{:S(2)}, u32[]{:S(2)}) collective-permute-start(f32[3,2,256,512]{3,2,1,0:T(8,128)S(1)} %get-tuple-element.846), channel_id=1, source_target_pairs={{0,1},{1,2},{2,3},{3,4},{4,5},{5,6},{6,7},{7,8},{8,9},{9,10},{10,1... | collective-permute-start | bytes 9437192 | tf_op jit(solution)/shard_map/ppermute | solution.py:25
  390.2 3.1 collective-permute-start.7
  393.3 66.7 %collective-permute-done.6 = f32[3,2,256,512]{3,2,1,0:T(8,128)S(1)} collective-permute-done((f32[3,2,256,512]{3,2,1,0:T(8,128)S(1)}, f32[3,2,256,512]{3,2,1,0:T(8,128)S(1)}, u32[]{:S(2)}, u32[]{:S(2)}) %collective-permute-start.6) | collective-permute-done | bytes 3145760 | tf_op jit(solution)/shard_map/ppermute | solution.py:25
  460.0 5.1 %multiply_subtract_fusion = f32[3,2,256,512]{3,2,1,0:T(8,128)} fusion(f32[3,2,256,512]{3,2,1,0:T(8,128)S(1)} %copy-done.3, f32[3,2,256,512]{3,2,1,0:T(8,128)S(1)} %collective-permute-done.7, f32[3,2,256,512]{3,2,1,0:T(8,128)S(1)} %collective-permute-done.6, f32[3,6,256,512]{3,2,1,0:T(8,128)} %get-tuple-element.592, f32[3]{0:T(128)S(1)} %copy-done.6), kind=kLoop, calls=%fused_computation.55 | loop fusion | flops 3145728 | bytes 15728652 | tf_op jit(solution)/shard_map/sub | solution.py:140
  (151 shorter events, 64.2 us)
Async XLA Ops:
  0.0 70.7 %copy-start = (f32[8,16]{1,0:T(8,128)S(1)}, f32[8,16]{1,0:T(8,128)}, u32[]{:S(2)}) copy-start(f32[8,16]{1,0:T(8,128)} %param.33) | copy-start | bytes 1540
  2.1 19.8 %collective-permute-start.1 = (bf16[3,2,256,512]{3,2,0,1:T(8,128)(2,1)S(1)}, bf16[3,2,256,512]{3,2,0,1:T(8,128)(2,1)}, u32[]{:S(2)}, u32[]{:S(2)}) collective-permute-start(bf16[3,2,256,512]{3,2,0,1:T(8,128)(2,1)S(1)} %copy.32), channel_id=1, source_target_pairs={{1,0},{2,1},{3,2},{4,3},{5,4},{6,5},{7,6},{8,7},{9,8},{10,9},{11,1... | collective-permute-start | bytes 4718600 | tf_op jit(solution)/shard_map/ppermute | solution.py:17
  4.0 37.7 %collective-permute-start = (bf16[3,2,256,512]{3,2,0,1:T(8,128)(2,1)S(1)}, bf16[3,2,256,512]{3,2,0,1:T(8,128)(2,1)}, u32[]{:S(2)}, u32[]{:S(2)}) collective-permute-start(bf16[3,2,256,512]{3,2,0,1:T(8,128)(2,1)S(1)} %copy.32), channel_id=1, source_target_pairs={{0,1},{1,2},{2,3},{3,4},{4,5},{5,6},{6,7},{7,8},{8,9},{9,10},{10,1... | collective-permute-start | bytes 4718600 | tf_op jit(solution)/shard_map/ppermute | solution.py:14
  7.8 39.8 %copy-start.1 = (bf16[2,256,1280]{2,1,0:T(8,128)(2,1)S(1)}, bf16[2,256,1280]{2,1,0:T(8,128)(2,1)}, u32[]{:S(2)}) copy-start(bf16[2,256,1280]{2,1,0:T(8,128)(2,1)} %param.28) | copy-start | bytes 3932164
  7.8 39.8 %copy-start.7 = (s32[1,4]{1,0:T(1,128)S(1)}, s32[1,4]{1,0:T(1,128)}, u32[]{:S(2)}) copy-start(s32[1,4]{1,0:T(1,128)} %param.31) | copy-start | bytes 52
  47.6 22.6 %copy-start.5 = (f32[16,3]{0,1:T(4,128)S(1)}, f32[16,3]{0,1:T(4,128)}, u32[]{:S(2)}) copy-start(f32[16,3]{0,1:T(4,128)} %param.34) | copy-start | bytes 580
  47.6 23.1 %copy-start.4 = (s32[1,8,4,1280]{3,2,1,0:T(4,128)S(1)}, s32[1,8,4,1280]{3,2,1,0:T(4,128)}, u32[]{:S(2)}) copy-start(s32[1,8,4,1280]{3,2,1,0:T(4,128)} %param.32) | copy-start | bytes 491524
  119.4 120.8 %copy-start.2 = (f32[3,2,256,512]{3,2,1,0:T(8,128)S(1)}, f32[3,2,256,512]{3,2,1,0:T(8,128)}, u32[]{:S(2)}) copy-start(f32[3,2,256,512]{3,2,1,0:T(8,128)} %param.26) | copy-start | bytes 9437188
  119.4 120.8 %copy-start.6 = (f32[3]{0:T(128)S(1)}, f32[3]{0:T(128)}, u32[]{:S(2)}) copy-start(f32[3]{0:T(128)} %param.35) | copy-start | bytes 40
  123.1 117.1 %collective-permute-start.2 = (f32[3,2,256,512]{3,2,1,0:T(8,128)S(1)}, f32[3,2,256,512]{3,2,1,0:T(8,128)S(1)}, u32[]{:S(2)}, u32[]{:S(2)}) collective-permute-start(f32[3,2,256,512]{3,2,1,0:T(8,128)S(1)} %get-tuple-element.848), channel_id=1, source_target_pairs={{0,1},{1,2},{2,3},{3,4},{4,5},{5,6},{6,7},{7,8},{8,9},{9,10},{10,1... | collective-permute-start | bytes 9437192 | tf_op jit(solution)/shard_map/ppermute | solution.py:25
  149.4 90.8 %collective-permute-start.3 = (f32[3,2,256,512]{3,2,1,0:T(8,128)S(1)}, f32[3,2,256,512]{3,2,1,0:T(8,128)S(1)}, u32[]{:S(2)}, u32[]{:S(2)}) collective-permute-start(f32[3,2,256,512]{3,2,1,0:T(8,128)S(1)} %get-tuple-element.849), channel_id=1, source_target_pairs={{1,0},{2,1},{3,2},{4,3},{5,4},{6,5},{7,6},{8,7},{9,8},{10,9},{11,1... | collective-permute-start | bytes 9437192 | tf_op jit(solution)/shard_map/ppermute | solution.py:25
  245.1 19.8 %collective-permute-start.5 = (bf16[3,2,256,512]{3,2,1,0:T(8,128)(2,1)S(1)}, bf16[3,2,256,512]{3,2,1,0:T(8,128)(2,1)}, u32[]{:S(2)}, u32[]{:S(2)}) collective-permute-start(bf16[3,2,256,512]{3,2,1,0:T(8,128)(2,1)S(1)} %get-tuple-element.844), channel_id=1, source_target_pairs={{1,0},{2,1},{3,2},{4,3},{5,4},{6,5},{7,6},{8,7},{9,8},{10,9},{11,1... | collective-permute-start | bytes 4718600 | tf_op jit(solution)/shard_map/ppermute | solution.py:17
  247.0 21.8 %collective-permute-start.4 = (bf16[3,2,256,512]{3,2,1,0:T(8,128)(2,1)S(1)}, bf16[3,2,256,512]{3,2,1,0:T(8,128)(2,1)}, u32[]{:S(2)}, u32[]{:S(2)}) collective-permute-start(bf16[3,2,256,512]{3,2,1,0:T(8,128)(2,1)S(1)} %get-tuple-element.844), channel_id=1, source_target_pairs={{0,1},{1,2},{2,3},{3,4},{4,5},{5,6},{6,7},{7,8},{8,9},{9,10},{10,1... | collective-permute-start | bytes 4718600 | tf_op jit(solution)/shard_map/ppermute | solution.py:14
  346.0 114.0 %copy-start.3 = (f32[3,2,256,512]{3,2,1,0:T(8,128)S(1)}, f32[3,2,256,512]{3,2,1,0:T(8,128)}, u32[]{:S(2)}) copy-start(f32[3,2,256,512]{3,2,1,0:T(8,128)} %get-tuple-element.845) | copy-start | bytes 9437188
  349.7 110.3 %collective-permute-start.6 = (f32[3,2,256,512]{3,2,1,0:T(8,128)S(1)}, f32[3,2,256,512]{3,2,1,0:T(8,128)S(1)}, u32[]{:S(2)}, u32[]{:S(2)}) collective-permute-start(f32[3,2,256,512]{3,2,1,0:T(8,128)S(1)} %get-tuple-element.846), channel_id=1, source_target_pairs={{0,1},{1,2},{2,3},{3,4},{4,5},{5,6},{6,7},{7,8},{8,9},{9,10},{10,1... | collective-permute-start | bytes 9437192 | tf_op jit(solution)/shard_map/ppermute | solution.py:25
  390.2 69.8 %collective-permute-start.7 = (f32[3,2,256,512]{3,2,1,0:T(8,128)S(1)}, f32[3,2,256,512]{3,2,1,0:T(8,128)S(1)}, u32[]{:S(2)}, u32[]{:S(2)}) collective-permute-start(f32[3,2,256,512]{3,2,1,0:T(8,128)S(1)} %get-tuple-element.847), channel_id=1, source_target_pairs={{1,0},{2,1},{3,2},{4,3},{5,4},{6,5},{7,6},{8,7},{9,8},{10,9},{11,1... | collective-permute-start | bytes 9437192 | tf_op jit(solution)/shard_map/ppermute | solution.py:25
where the time goes:
time: 473 us; the launch traced here: 465 us
  waiting for transfers between devices  194 us (41%)
  starting transfers between devices  95.7 us (20%)
  local copies, waits for them, and re-layouts  74 us (16%)
  loops' own time  67.8 us (14%)
  other arithmetic  18.5 us (4%)
  matrix products  13.9 us (3%)
    ppermute x4, waiting for transfers between devices, shifted(): return lax.ppermute(x, axis, pairs)  140 us
    ppermute x4, starting transfers between devices, shifted(): return lax.ppermute(x, axis, pairs)  86.8 us
    another operation x2, loops' own time, local(): summed, unused = lax.scan(accumulate, empty, slot_numbers)  36 us
    ppermute x2, waiting for transfers between devices, extended_2(): lax.ppermute(lax.slice_in_dim(block, 0, width, axis=dim), axis, backward)  29.5 us
    ppermute x2, waiting for transfers between devices, extended_2(): lax.ppermute(lax.slice_in_dim(block, block.shape[dim] - width, None, axis...  23.7 us
    another operation x2, loops' own time, local(): pieces = lax.map(project, slot_numbers)  19.7 us
    squeeze x8, local copies, waits for them, and re-layouts, accumulate(): current = lax.dynamic_index_in_dim(summed, where, 1, keepdims=False)  12.3 us
    dynamic_update_slice x8, local copies, waits for them, and re-layouts, accumulate(): return (lax.dynamic_update_index_in_dim(summed, added, where, 1), None)  10.6 us
  transfers between devices with their start and end apart: 8, of which 6 were waited for; matrix products, arithmetic and copies ran while one was open for 0% of the time, Pallas kernels for 0%

commit v1 on v0

v1 whole, which is shorter than its diff:
```python
import functools

import jax
import jax.numpy as jnp
from jax import lax
from jax.experimental import pallas as pl
from jax.experimental.pallas import tpu as pltpu
from jax.sharding import PartitionSpec as P

ITERS = 2
MESH = pl.DeviceIdType.MESH
F32 = jnp.float32
BF16 = jnp.bfloat16


def kernel(
    n,
    start_ref,
    count_ref,
    tiles_ref,
    spec_ref,
    atten_ref,
    step_ref,
    mats_ref,
    col_ref,
    row_ref,
    counts_ref,
    out_ref,
    rounded,
    lines,
    line_rows,
    line_pack,
    count_pack,
    grad_pack,
    grad_rows,
    grad_send,
    grad_recv,
    grad_sum,
    line_send_sem,
    line_recv_sem,
    grad_send_sem,
    grad_recv_sem,
):
    me = lax.axis_index("view")
    mats, own, height, width = mats_ref.shape
    tiles, _, columns = col_ref.shape
    window = tiles_ref.shape[1]
    bins, energies = spec_ref.shape
    pairs = own * tiles
    half = columns // 2
    has_low, has_high = me > 0, me < n - 1
    low, high = jnp.maximum(me - 1, 0), jnp.minimum(me + 1, n - 1)

    barrier = pltpu.get_barrier_semaphore()

    @pl.when(has_low)
    def _():
        pl.semaphore_signal(barrier, inc=1, device_id={"view": low}, device_id_type=MESH)

    @pl.when(has_high)
    def _():
        pl.semaphore_signal(barrier, inc=1, device_id={"view": high}, device_id_type=MESH)

    @pl.when(jnp.logical_not(has_low))
    def _():
        for it in range(ITERS):
            grad_recv[it, 0] = jnp.zeros(grad_recv.shape[2:], BF16)
            lines[it, 0:pairs] = jnp.zeros((pairs, mats, columns), F32)

    @pl.when(jnp.logical_not(has_high))
    def _():
        for it in range(ITERS):
            grad_recv[it, 1] = jnp.zeros(grad_recv.shape[2:], BF16)
            lines[it, 2 * pairs : 3 * pairs] = jnp.zeros((pairs, mats, columns), F32)

    def line_copy(it, way, s):
        landing = 0 if way == 0 else 2 * pairs
        return pltpu.make_async_remote_copy(
            src_ref=lines.at[it, pl.ds(pairs + s * tiles, tiles)],
            dst_ref=lines.at[it, pl.ds(landing + s * tiles, tiles)],
            send_sem=line_send_sem.at[it, way, s],
            recv_sem=line_recv_sem.at[it, way, s],
            device_id={"view": high if way == 0 else low},
            device_id_type=MESH,
        )

    def grad_copy(it, way):
        leaving = 2 * pairs if way == 0 else 0
        return pltpu.make_async_remote_copy(
            src_ref=grad_send.at[it, pl.ds(leaving, pairs)],
            dst_ref=grad_recv.at[it, way],
            send_sem=grad_send_sem.at[it, way],
            recv_sem=grad_recv_sem.at[it, way],
            device_id={"view": high if way == 0 else low},
            device_id_type=MESH,
        )

    sends = ((0, has_high), (1, has_low))
    receives = ((0, has_low), (1, has_high))

    for e in range(bins):
        c = counts_ref[0, e].astype(F32)
        count_pack[e] = jnp.concatenate([c[:, :half], c[:, half:]], axis=0)

    for s in range(own):
        for m in range(mats):
            rounded[s, m] = mats_ref[m, s].astype(BF16)

    first = start_ref[0] - (me * own - own)
    number = count_ref[0]

    for it in range(ITERS):
        for s in range(own):

            def chunk(i, _, s=s):
                cols = pl.ds(pl.multiple_of(i * 256, 256), 256)
                block = rounded[s].reshape(mats * height, width)
                for t in range(tiles):
                    across = jnp.dot(block, col_ref[t, :, cols], preferred_element_type=F32)
                    across = across.reshape(mats, height, 256) * row_ref[t, :, cols].astype(F32)[None]
                    lines[it, pairs + s * tiles + t, :, cols] = jnp.sum(across, axis=1)
                return 0

            lax.fori_loop(0, columns // 256, chunk, 0)
            if it == 0 and s == 0:
                pl.semaphore_wait(barrier, has_low.astype(jnp.int32) + has_high.astype(jnp.int32))

            for way, there in sends:

                @pl.when(there)
                def _(way=way, s=s):
                    line_copy(it, way, s).start()

        for s in range(own):
            for way, there in receives:

                @pl.when(there)
                def _(way=way, s=s):
                    line_copy(it, way, s).wait_recv()

        for j in range(window):
            at = jnp.clip(first + j, 0, 3 * own - 1) * tiles + tiles_ref[0, j]
            line_rows[j] = jnp.where(j < number, lines[it, at], 0.0)
        for m in range(mats):
            x = line_rows[:, m, :]
            line_pack[m] = jnp.concatenate([x[:, :half], x[:, half:]], axis=0)

        def poisson(i, _):
            cols = pl.ds(pl.multiple_of(i * 128, 128), 128)
            xs = [line_pack[m, :, cols] for m in range(mats)]
            trans = []
            for k in range(energies):
                total = atten_ref[k, 0] * xs[0]
                for m in range(1, mats):
                    total = total + atten_ref[k, m] * xs[m]
                trans.append(jnp.exp(-total))
            back = [None] * energies
            for e in range(bins):
                expected = spec_ref[e, 0] * trans[0]
                for k in range(1, energies):
                    expected = expected + spec_ref[e, k] * trans[k]
                weight = 1.0 - count_pack[e, :, cols] / expected
                for k in range(energies):
                    term = spec_ref[e, k] * weight
                    back[k] = term if e == 0 else back[k] + term
            for m in range(mats):
                total = None
                for k in range(energies):
                    term = atten_ref[k, m] * (trans[k] * back[k])
                    total = term if k == 0 else total + term
                grad_pack[m, :, cols] = -total
            return 0

        lax.fori_loop(0, half // 128, poisson, 0)
        for m in range(mats):
            y = grad_pack[m]
            grad_rows[:, m, :] = jnp.concatenate([y[:window], y[window:]], axis=1)
        for place in list(range(own)) + list(range(2 * own, 3 * own)) + list(range(own, 2 * own)):
            j = place - first
            held = (j >= 0) & (j < number)
            j = jnp.clip(j, 0, window - 1)
            value = grad_rows[j]
            tile = tiles_ref[0, j]
            for t in range(tiles):
                grad_send[it, place * tiles + t] = jnp.where(held & (tile == t), value, 0.0).astype(BF16)
        for way, there in sends:

            @pl.when(there)
            def _(way=way):
                grad_copy(it, way).start()

        for way, there in receives:

            @pl.when(there)
            def _(way=way):
                grad_copy(it, way).wait_recv()

        grad_sum[...] = (
            grad_send[it, pairs : 2 * pairs].astype(F32)
            + grad_recv[it, 0].astype(F32)
            + grad_recv[it, 1].astype(F32)
        )

        before = mats_ref if it == 0 else out_ref

        def back_step(s, _):
            for m in range(mats):
                total = None
                for t in range(tiles):
                    g = grad_sum[s * tiles + t][m : m + 1]
                    weighted = (g * row_ref[t].astype(F32)).astype(BF16)
                    part = lax.dot_general(
                        weighted, col_ref[t], (((1,), (1,)), ((), ())), preferred_element_type=F32
                    )
                    total = part if t == 0 else total + part
                new = before[m, s] - step_ref[m] * total
                out_ref[m, s] = new
                if it < ITERS - 1:
                    rounded[s, m] = new.astype(BF16)
            return 0

        lax.fori_loop(0, own, back_step, 0)

    for it in range(ITERS):
        for way, there in sends:

            @pl.when(there)
            def _(way=way, it=it):
                for s in range(own):
                    line_copy(it, way, s).wait_send()
                grad_copy(it, way).wait_send()


def solution(mesh):
    n = mesh.shape["view"]

    def local(materials, column_profile, row_profile, start, count, tile_ids, counts, spectrum, attenuation, step):
        mats, own, height, width = materials.shape
        tiles, _, columns = column_profile.shape
        views, window = tile_ids.shape
        bins = spectrum.shape[0]
        assert views == 1
        pairs = own * tiles
        vmem = pl.BlockSpec(memory_space=pltpu.VMEM)
        smem = pl.BlockSpec(memory_space=pltpu.SMEM)
        return pl.pallas_call(
            functools.partial(kernel, n),
            out_shape=jax.ShapeDtypeStruct(materials.shape, F32),
            in_specs=[smem] * 6 + [vmem] * 4,
            out_specs=vmem,
            scratch_shapes=[
                pltpu.VMEM((own, mats, height, width), BF16),
                pltpu.VMEM((ITERS, 3 * pairs, mats, columns), F32),
                pltpu.VMEM((window, mats, columns), F32),
                pltpu.VMEM((mats, 2 * window, columns // 2), F32),
                pltpu.VMEM((bins, 2 * window, columns // 2), F32),
                pltpu.VMEM((mats, 2 * window, columns // 2), F32),
                pltpu.VMEM((window, mats, columns), F32),
                pltpu.VMEM((ITERS, 3 * pairs, mats, columns), BF16),
                pltpu.VMEM((ITERS, 2, pairs, mats, columns), BF16),
                pltpu.VMEM((pairs, mats, columns), F32),
                pltpu.SemaphoreType.DMA((ITERS, 2, own)),
                pltpu.SemaphoreType.DMA((ITERS, 2, own)),
                pltpu.SemaphoreType.DMA((ITERS, 2)),
                pltpu.SemaphoreType.DMA((ITERS, 2)),
            ],
            compiler_params=pltpu.CompilerParams(
                collective_id=0, has_side_effects=True, vmem_limit_bytes=56 * 1024 * 1024
            ),
        )(start, count, tile_ids, spectrum, attenuation, step, materials, column_profile, row_profile, counts)

    placed = (
        P(None, ("groups", "view"), None, None),
        P(),
        P(),
        P(("groups", "view")),
        P(("groups", "view")),
        P(("groups", "view"), None),
        P(("groups", "view"), None, None, None),
        P(),
        P(),
        P(),
    )
    return jax.shard_map(
        local,
        mesh=mesh,
        in_specs=placed,
        out_specs=P(None, ("groups", "view"), None, None),
        check_vma=False,
    )
```

time: 473 us -> 46.8 us (0.10)
  the two profiles are of different devices: /device:TPU:6 before, /device:TPU:5 now
where the time goes in v1:
time: 46.8 us; the launch traced here: 46.6 us
  Pallas kernels  39.8 us (85%)
  local copies, waits for them, and re-layouts  5.49 us (12%)
  between operations  1.31 us (3%)
    pallas_call x1, Pallas kernels, local(): pl.pallas_call(functools.partial(kernel, n), out_shape=jax.ShapeDtypeStru...  39.8 us
    unnamed x2, local copies, waits for them, and re-layouts  5.49 us

profile of v1, /device:TPU:5, one launch (start us, length us, event | category | flops | bytes accessed | tf_op | source)
XLA Modules:
  0.0 46.6 jit_solution(11945761987925425298)
XLA Ops:
  1.3 1.4 %copy.11.atten_ref = f32[16,3]{1,0:T(8,128)} copy(f32[16,3]{0,1:T(4,128)} %param.18) | data formatting | bytes 384 | tf_op args[8]
  2.7 39.8 %shard_map.100 = f32[3,2,256,512]{3,2,1,0:T(8,128)} custom-call(s32[1]{0:T(128)S(6)} %copy.13.start_ref, s32[1]{0:T(128)S(6)} %copy.14.count_ref, s32[1,4]{1,0:T(1,128)} %tiles_ref.1, f32[8,16]{1,0:T(8,128)} %spec_ref.1, f32[16,3]{1,0:T(8,128)} %copy.11.atten_ref, f32[3]{0:T(128)} %step_ref.1, f32[3,2,256,512]{3,2,1,0:T(8,128)} %mats_ref.1, ...), custom_call_target="tpu_custom_call" | custom-call | tf_op jit(solution)/shard_map/pallas_call | solution.py:246
  42.4 4.1 %copy.15 = f32[3,2,256,512]{3,2,1,0:T(8,128)} copy(f32[3,2,256,512]{3,2,1,0:T(8,128)} %shard_map.100) | data formatting | bytes 6291456

commit v2 on v1

--- a/solution.py
+++ b/solution.py
@@ -11,6 +11,24 @@
 MESH = pl.DeviceIdType.MESH
 F32 = jnp.float32
 BF16 = jnp.bfloat16
+
+
+def back_projected(mats, tiles, s, grad_ref, row_ref, col_ref):
+    total = None
+    for t in range(tiles):
+        g = grad_ref[s * tiles + t]
+        profile = row_ref[t].astype(F32)
+        weighted = jnp.concatenate([(g[m : m + 1] * profile).astype(BF16) for m in range(mats)], axis=0)
+        part = lax.dot_general(weighted, col_ref[t], (((1,), (1,)), ((), ())), preferred_element_type=F32)
+        total = part if t == 0 else total + part
+    return total
+
+
+def final_kernel(step_ref, grad_ref, col_ref, row_ref, mats_ref, out_ref):
+    mats, _, height, _ = mats_ref.shape
+    total = back_projected(mats, col_ref.shape[0], pl.program_id(0), grad_ref, row_ref, col_ref)
+    for m in range(mats):
+        out_ref[m, 0] = mats_ref[m, 0] - step_ref[m] * total[m * height : (m + 1) * height]
 
 
 def kernel(
@@ -25,7 +43,11 @@
     col_ref,
     row_ref,
     counts_ref,
-    out_ref,
+    grad_sum,
+    mats_out,
+    maps,
+    column,
+    row,
     rounded,
     lines,
     line_rows,
@@ -35,7 +57,9 @@
     grad_rows,
     grad_send,
     grad_recv,
-    grad_sum,
+    load_sem,
+    chunk_sem,
+    store_sem,
     line_send_sem,
     line_recv_sem,
     grad_send_sem,
@@ -51,6 +75,24 @@
     has_low, has_high = me > 0, me < n - 1
     low, high = jnp.maximum(me - 1, 0), jnp.minimum(me + 1, n - 1)
 
+    def maps_load(s):
+        return pltpu.make_async_copy(mats_ref.at[:, s], maps.at[s], load_sem.at[s])
+
+    def chunk_load(which, i):
+        cols = pl.ds(pl.multiple_of(i * 256, 256), 256)
+        source, target = ((col_ref, column), (row_ref, row))[which]
+        return pltpu.make_async_copy(source.at[:, :, cols], target.at[:, :, cols], chunk_sem.at[which, i])
+
+    def maps_store(s):
+        return pltpu.make_async_copy(maps.at[s], mats_out.at[:, s], store_sem.at[s])
+
+    maps_load(0).start()
+    for i in range(columns // 256):
+        chunk_load(0, i).start()
+        chunk_load(1, i).start()
+    for s in range(1, own):
+        maps_load(s).start()
+
     barrier = pltpu.get_barrier_semaphore()
 
     @pl.when(has_low)
@@ -102,22 +144,25 @@
         c = counts_ref[0, e].astype(F32)
         count_pack[e] = jnp.concatenate([c[:, :half], c[:, half:]], axis=0)
 
-    for s in range(own):
-        for m in range(mats):
-            rounded[s, m] = mats_ref[m, s].astype(BF16)
-
     first = start_ref[0] - (me * own - own)
     number = count_ref[0]
 
     for it in range(ITERS):
         for s in range(own):
+            if it == 0:
+                maps_load(s).wait()
+                for m in range(mats):
+                    rounded[s, m] = maps[s, m].astype(BF16)
 
             def chunk(i, _, s=s):
+                if it == 0 and s == 0:
+                    chunk_load(0, i).wait()
+                    chunk_load(1, i).wait()
                 cols = pl.ds(pl.multiple_of(i * 256, 256), 256)
                 block = rounded[s].reshape(mats * height, width)
                 for t in range(tiles):
-                    across = jnp.dot(block, col_ref[t, :, cols], preferred_element_type=F32)
-                    across = across.reshape(mats, height, 256) * row_ref[t, :, cols].astype(F32)[None]
+                    across = jnp.dot(block, column[t, :, cols], preferred_element_type=F32)
+                    across = across.reshape(mats, height, 256) * row[t, :, cols].astype(F32)[None]
                     lines[it, pairs + s * tiles + t, :, cols] = jnp.sum(across, axis=1)
                 return 0
 
@@ -150,9 +195,9 @@
             xs = [line_pack[m, :, cols] for m in range(mats)]
             trans = []
             for k in range(energies):
-                total = atten_ref[k, 0] * xs[0]
+                total = atten_ref[0, k] * xs[0]
                 for m in range(1, mats):
-                    total = total + atten_ref[k, m] * xs[m]
+                    total = total + atten_ref[m, k] * xs[m]
                 trans.append(jnp.exp(-total))
             back = [None] * energies
             for e in range(bins):
@@ -166,7 +211,7 @@
             for m in range(mats):
                 total = None
                 for k in range(energies):
-                    term = atten_ref[k, m] * (trans[k] * back[k])
+                    term = atten_ref[m, k] * (trans[k] * back[k])
                     total = term if k == 0 else total + term
                 grad_pack[m, :, cols] = -total
             return 0
@@ -201,26 +246,23 @@
             + grad_recv[it, 1].astype(F32)
         )
 
-        before = mats_ref if it == 0 else out_ref
-
-        def back_step(s, _):
-            for m in range(mats):
-                total = None
-                for t in range(tiles):
-                    g = grad_sum[s * tiles + t][m : m + 1]
-                    weighted = (g * row_ref[t].astype(F32)).astype(BF16)
-                    part = lax.dot_general(
-                        weighted, col_ref[t], (((1,), (1,)), ((), ())), preferred_element_type=F32
-                    )
-                    total = part if t == 0 else total + part
-                new = before[m, s] - step_ref[m] * total
-                out_ref[m, s] = new
-                if it < ITERS - 1:
+        if it < ITERS - 1:
+
+            def back_step(s, _):
+                total = back_projected(mats, tiles, s, grad_sum, row, column)
+                for m in range(mats):
+                    new = maps[s, m] - step_ref[m] * total[m * height : (m + 1) * height]
+                    maps[s, m] = new
                     rounded[s, m] = new.astype(BF16)
-            return 0
-
-        lax.fori_loop(0, own, back_step, 0)
-
+                return 0
+
+            lax.fori_loop(0, own, back_step, 0)
+            if it == ITERS - 2:
+                for s in range(own):
+                    maps_store(s).start()
+
+    for s in range(own):
+        maps_store(s).wait()
     for it in range(ITERS):
         for way, there in sends:
 
@@ -243,12 +285,19 @@
         pairs = own * tiles
         vmem = pl.BlockSpec(memory_space=pltpu.VMEM)
         smem = pl.BlockSpec(memory_space=pltpu.SMEM)
-        return pl.pallas_call(
+        anywhere = pl.BlockSpec(memory_space=pl.ANY)
+        grads, maps = pl.pallas_call(
             functools.partial(kernel, n),
-            out_shape=jax.ShapeDtypeStruct(materials.shape, F32),
-            in_specs=[smem] * 6 + [vmem] * 4,
-            out_specs=vmem,
+            out_shape=[
+                jax.ShapeDtypeStruct((pairs, mats, columns), F32),
+                jax.ShapeDtypeStruct(materials.shape, F32),
+            ],
+            in_specs=[smem] * 6 + [anywhere] * 3 + [vmem],
+            out_specs=[vmem, anywhere],
             scratch_shapes=[
+                pltpu.VMEM((own, mats, height, width), F32),
+                pltpu.VMEM(column_profile.shape, BF16),
+                pltpu.VMEM(row_profile.shape, BF16),
                 pltpu.VMEM((own, mats, height, width), BF16),
                 pltpu.VMEM((ITERS, 3 * pairs, mats, columns), F32),
                 pltpu.VMEM((window, mats, columns), F32),
@@ -258,7 +307,9 @@
                 pltpu.VMEM((window, mats, columns), F32),
                 pltpu.VMEM((ITERS, 3 * pairs, mats, columns), BF16),
                 pltpu.VMEM((ITERS, 2, pairs, mats, columns), BF16),
-                pltpu.VMEM((pairs, mats, columns), F32),
+                pltpu.SemaphoreType.DMA((own,)),
+                pltpu.SemaphoreType.DMA((2, columns // 256)),
+                pltpu.SemaphoreType.DMA((own,)),
                 pltpu.SemaphoreType.DMA((ITERS, 2, own)),
                 pltpu.SemaphoreType.DMA((ITERS, 2, own)),
                 pltpu.SemaphoreType.DMA((ITERS, 2)),
@@ -267,7 +318,16 @@
             compiler_params=pltpu.CompilerParams(
                 collective_id=0, has_side_effects=True, vmem_limit_bytes=56 * 1024 * 1024
             ),
-        )(start, count, tile_ids, spectrum, attenuation, step, materials, column_profile, row_profile, counts)
+        )(start, count, tile_ids, spectrum, attenuation.T, step, materials, column_profile, row_profile, counts)
+        slab = pl.BlockSpec((mats, 1, height, width), lambda s: (0, s, 0, 0))
+        return pl.pallas_call(
+            final_kernel,
+            grid=(own,),
+            out_shape=jax.ShapeDtypeStruct(materials.shape, F32),
+            in_specs=[smem, vmem, vmem, vmem, slab],
+            out_specs=slab,
+            compiler_params=pltpu.CompilerParams(vmem_limit_bytes=56 * 1024 * 1024),
+        )(step, grads, column_profile, row_profile, maps)
 
     placed = (
         P(None, ("groups", "view"), None, None),

time: 46.8 us -> 44.3 us (0.947)
  local copies, waits for them, and re-layouts: 5.49 us -> 0 us
  Pallas kernels: 39.8 us -> 42.8 us
    unnamed x2 -> x0, local copies, waits for them, and re-layouts: 5.49 us -> none
    pallas_call x1 -> x2, Pallas kernels: 39.8 us -> 42.8 us  [the longest x1 34.5 us: local(): pl.pallas_call(functools.partial(kernel, n), out_shape=[jax.ShapeDtypeStr...]
where the time goes in v2:
time: 44.3 us; the launch traced here: 44.1 us
  Pallas kernels  42.8 us (97%)
  between operations  1.3 us (3%)
    pallas_call x1, Pallas kernels, local(): pl.pallas_call(functools.partial(kernel, n), out_shape=[jax.ShapeDtypeStr...  34.5 us
    pallas_call x1, Pallas kernels, local(): pl.pallas_call(final_kernel, grid=(own,), out_shape=jax.ShapeDtypeStruct(...  8.27 us

profile of v2, /device:TPU:5, one launch (start us, length us, event | category | flops | bytes accessed | tf_op | source)
XLA Modules:
  0.0 44.1 jit_solution(4500470751439165799)
XLA Ops:
  1.3 34.5 %shard_map.100 = (f32[4,3,1280]{2,1,0:T(4,128)}, f32[3,2,256,512]{3,2,1,0:T(8,128)}) custom-call(s32[1]{0:T(128)S(6)} %copy.11.start_ref, s32[1]{0:T(128)S(6)} %copy.12.count_ref, s32[1,4]{1,0:T(1,128)} %tiles_ref.1, f32[8,16]{1,0:T(8,128)} %spec_ref.1, f32[3,16]{1,0:T(4,128)} %bitcast.1, f32[3]{0:T(128)} %step_ref.3, f32[3,2,256,512]{3,2,1,0:T(8,128)} %mats_ref.1, ...), custom_call_target="tpu_custom_call" | custom-call | tf_op jit(solution)/shard_map/pallas_call | solution.py:289
  35.8 8.3 %shard_map.101 = f32[3,2,256,512]{3,2,1,0:T(8,128)} custom-call(f32[3]{0:T(128)} %step_ref.3, f32[4,3,1280]{2,1,0:T(4,128)} %get-tuple-element.7.grad_ref, bf16[2,512,1280]{2,1,0:T(8,128)(2,1)} %col_ref.3, bf16[2,256,1280]{2,1,0:T(8,128)(2,1)} %row_ref.3, f32[3,2,256,512]{3,2,1,0:T(8,128)} %get-tuple-element.8.mats_ref), custom_call_target="tpu_custom_call" | custom-call | tf_op jit(solution)/shard_map/pallas_call | solution.py:323

commit v3 on v2

--- a/solution.py
+++ b/solution.py
@@ -24,11 +24,46 @@
     return total
 
 
-def final_kernel(step_ref, grad_ref, col_ref, row_ref, mats_ref, out_ref):
-    mats, _, height, _ = mats_ref.shape
-    total = back_projected(mats, col_ref.shape[0], pl.program_id(0), grad_ref, row_ref, col_ref)
-    for m in range(mats):
-        out_ref[m, 0] = mats_ref[m, 0] - step_ref[m] * total[m * height : (m + 1) * height]
+def final_kernel(
+    step_ref, grad_ref, col_ref, row_ref, mats_ref, out_ref, column, row, maps, new, tile_sem, load_sem, store_sem
+):
+    mats, own, height, _ = mats_ref.shape
+    tiles = col_ref.shape[0]
+    loads = [
+        (
+            pltpu.make_async_copy(row_ref.at[t], row.at[t], tile_sem.at[0, t]),
+            pltpu.make_async_copy(col_ref.at[t], column.at[t], tile_sem.at[1, t]),
+        )
+        for t in range(tiles)
+    ]
+    slices = [pltpu.make_async_copy(mats_ref.at[:, s], maps.at[s], load_sem.at[s]) for s in range(own)]
+    stores = [
+        [pltpu.make_async_copy(new.at[s, m], out_ref.at[m, s], store_sem.at[s, m]) for m in range(mats)]
+        for s in range(own)
+    ]
+    for pair in loads:
+        for copy in pair:
+            copy.start()
+    for copy in slices:
+        copy.start()
+    for s in range(own):
+        total = None
+        for t in range(tiles):
+            if s == 0:
+                for copy in loads[t]:
+                    copy.wait()
+            g = grad_ref[s * tiles + t]
+            profile = row[t].astype(F32)
+            weighted = jnp.concatenate([(g[m : m + 1] * profile).astype(BF16) for m in range(mats)], axis=0)
+            part = lax.dot_general(weighted, column[t], (((1,), (1,)), ((), ())), preferred_element_type=F32)
+            total = part if t == 0 else total + part
+        slices[s].wait()
+        for m in range(mats):
+            new[s, m] = maps[s, m] - step_ref[m] * total[m * height : (m + 1) * height]
+            stores[s][m].start()
+    for group in stores:
+        for copy in group:
+            copy.wait()
 
 
 def kernel(
@@ -166,7 +201,7 @@
                     lines[it, pairs + s * tiles + t, :, cols] = jnp.sum(across, axis=1)
                 return 0
 
-            lax.fori_loop(0, columns // 256, chunk, 0)
+            lax.fori_loop(0, columns // 256, chunk, 0, unroll=it > 0 or s > 0)
             if it == 0 and s == 0:
                 pl.semaphore_wait(barrier, has_low.astype(jnp.int32) + has_high.astype(jnp.int32))
 
@@ -216,7 +251,7 @@
                 grad_pack[m, :, cols] = -total
             return 0
 
-        lax.fori_loop(0, half // 128, poisson, 0)
+        lax.fori_loop(0, half // 128, poisson, 0, unroll=True)
         for m in range(mats):
             y = grad_pack[m]
             grad_rows[:, m, :] = jnp.concatenate([y[:window], y[window:]], axis=1)
@@ -319,13 +354,20 @@
                 collective_id=0, has_side_effects=True, vmem_limit_bytes=56 * 1024 * 1024
             ),
         )(start, count, tile_ids, spectrum, attenuation.T, step, materials, column_profile, row_profile, counts)
-        slab = pl.BlockSpec((mats, 1, height, width), lambda s: (0, s, 0, 0))
         return pl.pallas_call(
             final_kernel,
-            grid=(own,),
             out_shape=jax.ShapeDtypeStruct(materials.shape, F32),
-            in_specs=[smem, vmem, vmem, vmem, slab],
-            out_specs=slab,
+            in_specs=[smem, vmem, anywhere, anywhere, anywhere],
+            out_specs=anywhere,
+            scratch_shapes=[
+                pltpu.VMEM(column_profile.shape, BF16),
+                pltpu.VMEM(row_profile.shape, BF16),
+                pltpu.VMEM((own, mats, height, width), F32),
+                pltpu.VMEM((own, mats, height, width), F32),
+                pltpu.SemaphoreType.DMA((2, tiles)),
+                pltpu.SemaphoreType.DMA((own,)),
+                pltpu.SemaphoreType.DMA((own, mats)),
+            ],
             compiler_params=pltpu.CompilerParams(vmem_limit_bytes=56 * 1024 * 1024),
         )(step, grads, column_profile, row_profile, maps)
 

time: 44.3 us -> 43.8 us (0.989)
  Pallas kernels: 42.8 us -> 42.1 us
    pallas_call x1, Pallas kernels: 34.5 us -> 32.4 us  [local(): pl.pallas_call(functools.partial(kernel, n), out_shape=[jax.ShapeDtypeStr...]
    pallas_call x1, Pallas kernels: 8.27 us -> 9.71 us  [local(): pl.pallas_call(final_kernel, out_shape=jax.ShapeDtypeStruct(materials.sha...]
where the time goes in v3:
time: 43.8 us; the launch traced here: 43.6 us
  Pallas kernels  42.1 us (96%)
  between operations  1.47 us (3%)
    pallas_call x1, Pallas kernels, local(): pl.pallas_call(functools.partial(kernel, n), out_shape=[jax.ShapeDtypeStr...  32.4 us
    pallas_call x1, Pallas kernels, local(): pl.pallas_call(final_kernel, out_shape=jax.ShapeDtypeStruct(materials.sha...  9.71 us

profile of v3, /device:TPU:5, one launch (start us, length us, event | category | flops | bytes accessed | tf_op | source)
XLA Modules:
  0.0 43.6 jit_solution(13394517816116180990)
XLA Ops:
  1.3 32.4 %shard_map.100 = (f32[4,3,1280]{2,1,0:T(4,128)}, f32[3,2,256,512]{3,2,1,0:T(8,128)}) custom-call(s32[1]{0:T(128)S(6)} %copy.11.start_ref, s32[1]{0:T(128)S(6)} %copy.12.count_ref, s32[1,4]{1,0:T(1,128)} %tiles_ref.1, f32[8,16]{1,0:T(8,128)} %spec_ref.1, f32[3,16]{1,0:T(4,128)} %bitcast.1, f32[3]{0:T(128)} %step_ref.3, f32[3,2,256,512]{3,2,1,0:T(8,128)} %mats_ref.1, ...), custom_call_target="tpu_custom_call" | custom-call | tf_op jit(solution)/shard_map/pallas_call | solution.py:324
  33.7 9.7 %shard_map.101 = f32[3,2,256,512]{3,2,1,0:T(8,128)} custom-call(f32[3]{0:T(128)} %step_ref.3, f32[4,3,1280]{2,1,0:T(4,128)} %get-tuple-element.7.grad_ref, bf16[2,512,1280]{2,1,0:T(8,128)(2,1)} %col_ref.3, bf16[2,256,1280]{2,1,0:T(8,128)(2,1)} %row_ref.3, f32[3,2,256,512]{3,2,1,0:T(8,128)} %get-tuple-element.8.mats_ref), custom_call_target="tpu_custom_call" | custom-call | tf_op jit(solution)/shard_map/pallas_call | solution.py:357
